TPU v7x, 32 devices: a whole 2x2x4 slice. The times are simulated.
32 devices in a mesh: wide: 8 (over z, y), narrow: 4 (over x, core).
Axes of the slice: x: 2, y: 2, z: 4, core: 2. Of those that a mesh axis runs over, the one named last changes fastest.
Arguments:
- old_fields: float32 [2048, 6, 16, 256], P(('wide', 'narrow')), may hold values from -6 to 6
- old_target: int32 [2048], P(('wide', 'narrow')), may hold values from 0 to 2047, as said below
- cut_flag: int32 [16, 8, 16], P('wide', 'narrow'), may hold values 0 or 1
- apertures: float32 [3, 256, 128, 256], P(None, 'wide', 'narrow'), may hold values from 0.2 to 1
- volume: float32 [256, 128, 256], P('wide', 'narrow'), may hold values from 0.5 to 1
- velocity: float32 [3, 256, 128, 256], P(None, 'wide', 'narrow'), may hold values from -4 to 4
- diffusivity: float32 [6], replicated, may hold values from 0.02 to 0.08
- coupling: float32 [6, 6], replicated, may hold values from -2.5 to 2.5
Outputs:
- adjoint_out: float32 [6, 256, 128, 256], P(None, 'wide', 'narrow')
Inputs may be any that keep to these rules, and one draw needn't show every extreme that they name: `old_target`: every new block is named by exactly one old block. The blocks held by one device go only to devices with the same narrow index, exactly 8 to each device of that wide row, itself included. A block's number is (bx * 8 + by) * 16 + bz and its new owner is the device with wide index bx / 2 and narrow index by / 2, rounded down.
All inputs are finite; a program needn't handle non-finite values. No bound on the sum of `cut_flag` on one device may be relied on, other than what follows from the above.
Results may differ from a plain program's by a relative error of at most 0.00012.
Values sent between devices are 32-bit elements; how exact they have to be, the bound alone decides.
No kernel may reach another device: no remote copies, remote signals or barrier semaphores. Data moves between devices by JAX's collectives and lax.ppermute only.
A program may use at most 320 MiB of HBM per device.

v0:
```python
import jax
import jax.numpy as jnp
from jax import lax
from jax.sharding import PartitionSpec as P

BE = 16
BPX = 2
BPY = 2
BPZ = 16


ADVECT = 0.2


def passed_along(value, axis, by):
    count = lax.axis_size(axis)
    pairs = [(i, i + by) for i in range(count) if 0 <= i + by < count]
    return lax.ppermute(value, axis, pairs)


def padded_2(block, sides, width):
    for axis, dim in sides:
        count = lax.axis_size(axis)
        forward = [(i, i + 1) for i in range(count - 1)]
        backward = [(target, source) for source, target in forward]
        low = lax.ppermute(
            lax.slice_in_dim(block, block.shape[dim] - width, None, axis=dim), axis, forward
        )
        high = lax.ppermute(lax.slice_in_dim(block, 0, width, axis=dim), axis, backward)
        block = jnp.concatenate([low, block, high], axis=dim)
    return block


def diffuse(padded, open_x, open_y, open_z):
    center = padded[:, 1:-1, 1:-1, :]
    line_x = padded[:, :, 1:-1, :]
    flux_x = open_x[None] * (line_x[:, 1:] - line_x[:, :-1])
    line_y = padded[:, 1:-1, :, :]
    flux_y = open_y[None] * (line_y[:, :, 1:] - line_y[:, :, :-1])
    line_z = jnp.pad(center, ((0, 0), (0, 0), (0, 0), (1, 1)))
    low_z = jnp.pad(open_z, ((0, 0), (0, 0), (1, 0)))
    flux_z = low_z[None] * (line_z[..., 1:] - line_z[..., :-1])
    return (
        flux_x[:, 1:]
        - flux_x[:, :-1]
        + (flux_y[:, :, 1:] - flux_y[:, :, :-1])
        + (flux_z[..., 1:] - flux_z[..., :-1])
    )


def advect(padded, carry_x, carry_y, carry_z):
    center = padded[:, 1:-1, 1:-1, :]
    line_x = padded[:, :, 1:-1, :]
    flux_x = carry_x[None] * (line_x[:, 1:] + line_x[:, :-1]) * 0.5
    line_y = padded[:, 1:-1, :, :]
    flux_y = carry_y[None] * (line_y[:, :, 1:] + line_y[:, :, :-1]) * 0.5
    line_z = jnp.pad(center, ((0, 0), (0, 0), (0, 0), (1, 1)))
    low_z = jnp.pad(carry_z, ((0, 0), (0, 0), (1, 0)))
    flux_z = low_z[None] * (line_z[..., 1:] + line_z[..., :-1]) * 0.5
    return (
        flux_x[:, 1:]
        - flux_x[:, :-1]
        + (flux_y[:, :, 1:] - flux_y[:, :, :-1])
        + (flux_z[..., 1:] - flux_z[..., :-1])
    )


def first_section(padded, geometry, viscous_rate):
    center = padded[:, 1:-1, 1:-1, :]
    return (
        center + viscous_rate * diffuse(padded, geometry[0], geometry[1], geometry[2]) / geometry[6]
    )


def second_section(padded, geometry):
    center = padded[:, 1:-1, 1:-1, :]
    return center - ADVECT * advect(padded, geometry[3], geometry[4], geometry[5]) / geometry[6]


def third_section(padded, geometry, viscous_rate, coupling):
    center = padded[:, 1:-1, 1:-1, :]
    mixed = jnp.einsum("cj,jxyz->cxyz", coupling, center, precision=lax.Precision.HIGHEST)
    return (
        center
        + viscous_rate * diffuse(padded, geometry[0], geometry[1], geometry[2]) / geometry[6]
        + mixed
    )


def assemble(placed):
    fields = placed.shape[1]
    shaped = placed.reshape(BPX, BPY, BPZ, fields, BE, BE, BE).transpose(3, 0, 4, 1, 5, 2, 6)
    return shaped.reshape(fields, BPX * BE, BPY * BE, BPZ * BE)


def slot_of(target_ids, grid_y):
    layer = grid_y * BPZ
    block_x = target_ids // layer
    remainder = target_ids % layer
    block_y = remainder // BPZ
    block_z = remainder % BPZ
    return (block_x % BPX * BPY + block_y % BPY) * BPZ + block_z


def inverse_of(new_slot, blocks):
    return jnp.zeros((blocks,), jnp.int32).at[new_slot].set(jnp.arange(blocks, dtype=jnp.int32))


def on_device(old_fields, old_target, cut_flag, apertures, volume, velocity, diffusivity, coupling):
    narrow_count = lax.axis_size("narrow")
    blocks = old_fields.shape[0]
    grid_y = BPY * narrow_count
    destination = old_target // (grid_y * BPZ) // BPX
    ordering = jnp.argsort(destination * blocks + jnp.arange(blocks, dtype=jnp.int32))
    outgoing = old_fields[ordering]
    out_ids = old_target[ordering]
    arrived, arrived_ids = (
        lax.all_to_all(outgoing, "wide", split_axis=0, concat_axis=0, tiled=True),
        lax.all_to_all(out_ids, "wide", split_axis=0, concat_axis=0, tiled=True),
    )
    invert = inverse_of(slot_of(arrived_ids, grid_y), blocks)
    adjoint = assemble(arrived[invert])
    cut_cells = jnp.repeat(jnp.repeat(jnp.repeat(cut_flag, BE, 0), BE, 1), BE, 2) > 0
    face_open = jnp.where(cut_cells[None], apertures, 1.0)
    volume_fill = jnp.where(cut_cells, volume, 1.0)
    transport = face_open * velocity
    viscous_rate = diffusivity[:, None, None, None]
    low_x = passed_along((face_open[0][-1:], transport[0][-1:]), "wide", 1)
    low_y = passed_along((face_open[1][:, -1:], transport[1][:, -1:]), "narrow", 1)
    open_x = jnp.concatenate([low_x[0], face_open[0]], 0)
    carry_x = jnp.concatenate([low_x[1], transport[0]], 0)
    open_y = jnp.concatenate([low_y[0], face_open[1]], 1)
    carry_y = jnp.concatenate([low_y[1], transport[1]], 1)
    geometry = (open_x, open_y, face_open[2], carry_x, carry_y, transport[2], volume_fill)

    def ghost(values):
        return padded_2(values, (("wide", 1), ("narrow", 2)), 1)

    after_one = first_section(ghost(adjoint), geometry, viscous_rate)
    after_two = second_section(ghost(after_one), geometry)
    return third_section(ghost(after_two), geometry, viscous_rate, coupling)


def solution(mesh):
    in_specs = (
        P(("wide", "narrow"), None, None, None),
        P(("wide", "narrow")),
        P("wide", "narrow", None),
        P(None, "wide", "narrow", None),
        P("wide", "narrow", None),
        P(None, "wide", "narrow", None),
        P(),
        P(),
    )
    out_specs = P(None, "wide", "narrow", None)
    return jax.shard_map(
        on_device, mesh=mesh, in_specs=in_specs, out_specs=out_specs, check_vma=False
    )
```

profile of v0, /device:TPU:21, one launch (start us, length us, event | category | flops | bytes accessed | tf_op | source)
XLA Modules:
  0.0 482.0 jit_solution(8092120627358094886)
XLA Ops:
  0.0 0.7 iota_add_fusion
  0.7 2.0 sort.17
  2.7 1.4 gather_fusion.1
  4.9 5.5 %all-to-all-start.1 = ((s32[8,8,1]{1,2,0:T(1,128)}), s32[8,8,1]{1,2,0:T(1,128)S(1)}, u32[]{:S(2)}, u32[]{:S(2)}) async-start(s32[8,8,1]{1,2,0:T(1,128)} %bitcast), calls=%async_computation.1 | async-start | bytes 8192 | tf_op jit(solution)/shard_map/all_to_all | solution.py:119
  10.4 6.4 %gather_fusion = f32[64,6,16,256]{3,2,1,0:T(8,128)} fusion(f32[64,6,16,256]{3,2,1,0:T(8,128)} %param.8, s32[1024]{0:T(1024)S(1)} %pad_clamp_fusion.1), kind=kCustom, calls=%fused_computation | custom fusion | bytes 12583168 | tf_op jit(solution)/shard_map/gather | solution.py:115
  16.8 5.6 %all-to-all-start = ((f32[64,6,16,256]{3,2,1,0:T(8,128)}), f32[64,6,16,256]{3,2,1,0:T(8,128)}, u32[]{:S(2)}, u32[]{:S(2)}) async-start(f32[64,6,16,256]{3,2,1,0:T(8,128)} %gather_fusion), calls=%async_computation | async-start | bytes 12582912 | tf_op jit(solution)/shard_map/all_to_all | solution.py:118
  23.1 1.4 copy.58
  24.5 3.7 fusion.43
  28.3 2.0 slice_bitcast_fusion.2
  30.3 4.8 collective-permute-start.3
  35.2 3.1 collective-permute-start
  38.3 2.2 collective-permute-start.9
  40.5 3.1 collective-permute-start.6
  43.6 2.8 copy.65
  46.4 5.0 %broadcast_select_fusion = f32[32,32,256]{1,2,0:T(8,128)} fusion(f32[32,32,256]{1,2,0:T(8,128)} %copy.65, pred[32,32,16]{1,2,0:T(8,128)(4,1)S(1)} %copy.57), kind=kLoop, calls=%fused_computation.71 | loop fusion | flops 262144 | bytes 2113536 | tf_op jit(solution)/shard_map/jit(_where)/select_n | solution.py:125
  51.4 3.6 copy.66
  55.0 1.7 pad.18
  56.7 1.6 pad.20
  59.0 0.7 reduce.3
  59.8 0.8 scatter_custom_fusion
  60.6 1.3 pad_maximum_fusion.14
  62.0 44.2 %collective-permute-done = f32[1,32,256]{2,1,0:T(8,128)S(1)} collective-permute-done((f32[1,32,256]{2,1,0:T(8,128)S(1)}, f32[1,32,256]{2,1,0:T(8,128)S(1)}, u32[]{:S(2)}, u32[]{:S(2)}) %collective-permute-start) | collective-permute-done | bytes 32800 | tf_op jit(solution)/shard_map/ppermute | solution.py:18
  106.2 2.3 pad_maximum_fusion.16
  108.6 2.4 pad_maximum_fusion.17
  111.0 2.4 pad_maximum_fusion.15
  113.4 43.7 %all-to-all-done = f32[64,6,16,256]{3,2,1,0:T(8,128)} async-done(((f32[64,6,16,256]{3,2,1,0:T(8,128)}), f32[64,6,16,256]{3,2,1,0:T(8,128)}, u32[]{:S(2)}, u32[]{:S(2)}) %all-to-all-start) | async-done | bytes 6291488 | tf_op jit(solution)/shard_map/all_to_all | solution.py:118
  157.1 6.4 %gather_fusion.2 = f32[64,6,16,256]{3,2,1,0:T(8,128)} fusion(f32[64,6,16,256]{3,2,1,0:T(8,128)} %all-to-all-done, s32[1024]{0:T(1024)S(1)} %pad_clamp_fusion), kind=kCustom, calls=%fused_computation.2 | custom fusion | bytes 12583168 | tf_op jit(solution)/shard_map/gather | solution.py:122
  163.5 28.9 %reshape.278 = f32[2,2,16,6,16,16,16]{6,5,4,3,2,1,0:T(8,128)} reshape(f32[64,6,16,256]{3,2,1,0:T(8,128)} %gather_fusion.2) | data formatting | bytes 12582912 | tf_op jit(solution)/shard_map/reshape | solution.py:92
  192.5 45.9 %copy.73 = f32[2,2,16,6,16,16,16]{6,2,5,1,4,0,3:T(8,128)} copy(f32[2,2,16,6,16,16,16]{6,5,4,3,2,1,0:T(8,128)} %reshape.278) | data formatting | bytes 12582912 | tf_op jit(solution)/shard_map/reshape | solution.py:92
  238.3 34.6 %reshape.279 = f32[6,32,32,256]{3,2,1,0:T(8,128)} reshape(f32[6,2,16,2,16,16,16]{6,5,4,3,2,1,0:T(8,128)} %bitcast.39) | data formatting | bytes 12582912 | tf_op jit(solution)/shard_map/reshape | solution.py:93
  272.9 8.5 %copy.67 = f32[6,32,32,256]{3,0,2,1:T(8,128)S(1)} copy(f32[6,32,32,256]{3,2,1,0:T(8,128)} %reshape.279) | data formatting | bytes 12582912 | tf_op jit(solution)/shard_map/reshape | solution.py:93
  281.4 6.1 %collective-permute-start.2 = (f32[6,1,32,256]{3,0,2,1:T(8,128)S(1)}, f32[6,1,32,256]{3,0,2,1:T(8,128)S(1)}, u32[]{:S(2)}, u32[]{:S(2)}) collective-permute-start(f32[6,1,32,256]{3,0,2,1:T(8,128)S(1)} %get-tuple-element.20), channel_id=1, source_target_pairs={{0,4},{4,8},{8,12},{12,16},{16,20},{20,24},{24,28},{1,5},{5,9},{9,... | collective-permute-start | bytes 589832 | tf_op jit(solution)/shard_map/ppermute | solution.py:26
  287.5 6.9 %fusion.1 = f32[6,32,32,257]{3,0,2,1:T(8,128)} fusion(f32[6,32,32,256]{3,0,2,1:T(8,128)S(1)} %copy.67, f32[32,32,257]{2,1,0:T(8,128)S(1)} %pad.18), kind=kLoop, calls=%fused_computation.12 | loop fusion | flops 3158016 | bytes 13660160 | tf_op jit(solution)/shard_map/mul | solution.py:42
  294.5 9.1 %collective-permute-start.1 = (f32[6,1,32,256]{3,0,2,1:T(8,128)S(1)}, f32[6,1,32,256]{3,0,2,1:T(8,128)S(1)}, u32[]{:S(2)}, u32[]{:S(2)}) collective-permute-start(f32[6,1,32,256]{3,0,2,1:T(8,128)S(1)} %get-tuple-element.19), channel_id=1, source_target_pairs={{4,0},{8,4},{12,8},{16,12},{20,16},{24,20},{28,24},{5,1},{9,5},{13... | collective-permute-start | bytes 589832 | tf_op jit(solution)/shard_map/ppermute | solution.py:29
  303.6 2.7 collective-permute-done.2
  306.3 0.7 constant_dynamic-update-slice_fusion.1
  307.1 8.7 %copy_dynamic-update-slice_fusion = f32[6,34,32,256]{3,0,2,1:T(8,128)} fusion(f32[6,34,32,256]{3,0,2,1:T(8,128)} %constant_dynamic-update-slice_fusion.1, f32[6,32,32,256]{3,2,1,0:T(8,128)S(1)} %bitcast.41), kind=kLoop, calls=%fused_computation.75 | loop fusion | bytes 14680064
  315.7 0.7 constant_dynamic-update-slice_fusion
  316.5 1.1 fusion.44
  317.6 4.2 collective-permute-start.5
  321.7 1.9 collective-permute-start.4
  323.7 4.7 fusion.14
  328.4 1.2 collective-permute-done.4
  329.6 11.3 %fusion.13 = f32[6,32,33,256]{3,0,2,1:T(8,128)} fusion(f32[6,34,32,256]{3,0,2,1:T(8,128)} %constant_dynamic-update-slice_fusion, f32[6,34,1,256]{3,0,2,1:T(8,128)S(1)} %collective-permute-done.5, f32[6,34,1,256]{3,0,2,1:T(8,128)S(1)} %collective-permute-done.4, f32[32,33,256]{2,1,0:T(8,128)S(1)} %pad_maximum_fusion.14), kind=kLoop, calls=%fused_computation.37 | loop fusion | flops 6488064 | bytes 14671872 | tf_op jit(solution)/shard_map/mul | solution.py:39
  341.0 20.5 %fusion.32 = f32[6,32,32,256]{3,0,2,1:T(8,128)S(1)} fusion(f32[6,32,32,257]{3,0,2,1:T(8,128)} %fusion.1, f32[6,32,33,256]{3,0,2,1:T(8,128)} %fusion.13, f32[6,33,32,256]{3,0,2,1:T(8,128)} %fusion.14, f32[32,32,256]{2,1,0:T(8,128)S(1)} %copy-done.7, f32[6]{0:T(128)S(1)} %copy-done.16, f32[6,32,32,256]{3,2,1,0:T(8,128)S(1)} %bitcast.41), kind=kLoop, calls=%fused_computation.67 | loop fusion | flops 12582912 | bytes 51380248 | tf_op jit(solution)/shard_map/add | solution.py:71
  361.5 1.9 collective-permute-start.7
  363.5 4.3 collective-permute-start.8
  367.7 6.7 %fusion.4 = f32[6,32,32,257]{3,0,2,1:T(8,128)} fusion(f32[6,32,32,256]{3,0,2,1:T(8,128)S(1)} %fusion.32, f32[32,32,257]{2,1,0:T(8,128)S(1)} %copy-done.9), kind=kLoop, calls=%fused_computation.15 | loop fusion | flops 4737024 | bytes 13660160 | tf_op jit(solution)/shard_map/mul | solution.py:59
  375.1 4.4 collective-permute-start.11
  379.5 2.1 collective-permute-start.10
  381.6 4.6 fusion.16
  386.2 1.3 collective-permute-done.10
  387.5 6.7 %fusion.11 = f32[6,32,33,256]{3,0,2,1:T(8,128)} fusion(f32[6,34,1,256]{3,0,2,1:T(8,128)S(1)} %collective-permute-done.11, f32[6,1,32,256]{3,0,2,1:T(8,128)S(1)} %collective-permute-done.7, f32[6,32,32,256]{3,0,2,1:T(8,128)S(1)} %fusion.32, f32[6,1,32,256]{3,0,2,1:T(8,128)S(1)} %collective-permute-done.8, f32[6,34,1,256]{3,0,2,1:T(8,128)S(1)} %collective-permute-done.10, ...), kind=kLoop, calls=%fused_computation.29 | loop fusion | flops 14598144 | bytes 14671872 | tf_op jit(solution)/shard_map/mul | solution.py:56
  394.2 18.4 %fusion.27 = f32[6,32,32,256]{3,0,2,1:T(8,128)S(1)} fusion(f32[6,32,32,256]{3,0,2,1:T(8,128)S(1)} %fusion.32, f32[6,32,32,257]{3,0,2,1:T(8,128)} %fusion.4, f32[6,32,33,256]{3,0,2,1:T(8,128)} %fusion.11, f32[6,33,32,256]{3,0,2,1:T(8,128)} %fusion.16, f32[32,32,256]{2,1,0:T(8,128)S(1)} %copy-done.8), kind=kLoop, calls=%fused_computation.59 | loop fusion | flops 12582912 | bytes 51380224 | tf_op jit(solution)/shard_map/sub | solution.py:77
  412.7 2.2 collective-permute-start.12
  414.8 4.3 collective-permute-start.13
  419.1 7.8 %fusion.6 = f32[6,32,32,257]{3,0,2,1:T(8,128)} fusion(f32[6,32,32,256]{3,0,2,1:T(8,128)S(1)} %fusion.27, f32[32,32,257]{2,1,0:T(8,128)} %copy-done.2), kind=kLoop, calls=%fused_computation.17 | loop fusion | flops 3158016 | bytes 13660160 | tf_op jit(solution)/shard_map/mul | solution.py:42
  426.9 3.6 collective-permute-start.15
  430.5 2.1 collective-permute-start.14
  432.6 4.5 fusion.17
  437.1 1.5 collective-permute-done.14
  438.5 6.5 %fusion.8 = f32[6,32,33,256]{3,0,2,1:T(8,128)} fusion(f32[6,34,1,256]{3,0,2,1:T(8,128)S(1)} %collective-permute-done.15, f32[6,1,32,256]{3,0,2,1:T(8,128)S(1)} %collective-permute-done.12, f32[6,32,32,256]{3,0,2,1:T(8,128)S(1)} %fusion.27, f32[6,1,32,256]{3,0,2,1:T(8,128)S(1)} %collective-permute-done.13, f32[6,34,1,256]{3,0,2,1:T(8,128)S(1)} %collective-permute-done.14, ...), kind=kLoop, calls=%fused_computation.20 | loop fusion | flops 12976128 | bytes 14671872 | tf_op jit(solution)/shard_map/mul | solution.py:39
  445.0 28.4 %fusion.22 = f32[6,32,32,256]{3,0,2,1:T(8,128)} fusion(f32[6,32,32,256]{3,0,2,1:T(8,128)} %copy-done.1, f32[6,32,32,257]{3,0,2,1:T(8,128)} %fusion.6, f32[6,32,33,256]{3,0,2,1:T(8,128)} %fusion.8, f32[6,33,32,256]{3,0,2,1:T(8,128)} %fusion.17, f32[32,32,256]{2,1,0:T(8,128)S(1)} %copy-done.8, f32[6]{0:T(128)S(1)} %copy-done.16, f32[6,6]{1,0:T(8,128)S(1)} %copy-done), kind=kOutput, calls=%fused_computation.51 | convolution fusion | flops 127401984 | bytes 74449064 | tf_op jit(solution)/shard_map/cj,jxyz->cxyz/dot_general | solution.py:82
  473.4 8.1 %copy.68 = f32[6,32,32,256]{3,2,1,0:T(8,128)} copy(f32[6,32,32,256]{3,0,2,1:T(8,128)} %fusion.22) | data formatting | bytes 12582912 | tf_op jit(solution)/shard_map/add | solution.py:84
  (77 shorter events, 3.0 us)
Async XLA Ops:
  0.0 445.0 %copy-start = (f32[6,6]{1,0:T(8,128)S(1)}, f32[6,6]{1,0:T(8,128)}, u32[]{:S(2)}) copy-start(f32[6,6]{1,0:T(8,128)} %param.15) | copy-start | bytes 436
  4.9 12.0 %all-to-all-start.1 = ((s32[8,8,1]{1,2,0:T(1,128)}), s32[8,8,1]{1,2,0:T(1,128)S(1)}, u32[]{:S(2)}, u32[]{:S(2)}) async-start(s32[8,8,1]{1,2,0:T(1,128)} %bitcast), calls=%async_computation.1 | async-start | bytes 8192 | tf_op jit(solution)/shard_map/all_to_all | solution.py:119
  16.8 5.6 %copy-start.15 = (s32[2,2,16]{2,1,0:T(2,128)S(1)}, s32[2,2,16]{2,1,0:T(2,128)}, u32[]{:S(2)}) copy-start(s32[2,2,16]{2,1,0:T(2,128)} %param.10) | copy-start | bytes 772
  16.8 140.3 %all-to-all-start = ((f32[64,6,16,256]{3,2,1,0:T(8,128)}), f32[64,6,16,256]{3,2,1,0:T(8,128)}, u32[]{:S(2)}, u32[]{:S(2)}) async-start(f32[64,6,16,256]{3,2,1,0:T(8,128)} %gather_fusion), calls=%async_computation | async-start | bytes 12582912 | tf_op jit(solution)/shard_map/all_to_all | solution.py:118
  28.3 15.4 %copy-start.14 = (f32[32,32,256]{2,1,0:T(8,128)S(1)}, f32[32,32,256]{2,1,0:T(8,128)}, u32[]{:S(2)}) copy-start(f32[32,32,256]{2,1,0:T(8,128)} %param.12) | copy-start | bytes 3145732
  30.3 10.2 %copy-start.11 = (f32[32,32,256]{2,1,0:T(8,128)}, f32[32,32,256]{2,1,0:T(8,128)S(1)}, u32[]{:S(2)}) copy-start(f32[32,32,256]{2,1,0:T(8,128)S(1)} %get-tuple-element.23) | copy-start | bytes 3145732
  30.3 10.2 %copy-start.12 = (f32[32,32,256]{2,1,0:T(8,128)}, f32[32,32,256]{2,1,0:T(8,128)S(1)}, u32[]{:S(2)}) copy-start(f32[32,32,256]{2,1,0:T(8,128)S(1)} %get-tuple-element.27) | copy-start | bytes 3145732
  30.3 30.3 %collective-permute-start.3 = (f32[32,1,256]{2,1,0:T(1,128)S(1)}, f32[32,1,256]{2,1,0:T(1,128)S(1)}, u32[]{:S(2)}, u32[]{:S(2)}) collective-permute-start(f32[32,1,256]{2,1,0:T(1,128)S(1)} %slice.262), channel_id=1, source_target_pairs={{0,1},{1,2},{2,3},{4,5},{5,6},{6,7},{8,9},{9,10},{10,11},{12,13},{... | collective-permute-start | bytes 98312 | tf_op jit(solution)/shard_map/ppermute | solution.py:18
  35.2 71.1 %collective-permute-start = (f32[1,32,256]{2,1,0:T(8,128)S(1)}, f32[1,32,256]{2,1,0:T(8,128)S(1)}, u32[]{:S(2)}, u32[]{:S(2)}) collective-permute-start(f32[1,32,256]{2,1,0:T(8,128)S(1)} %slice_bitcast_fusion.7), channel_id=1, source_target_pairs={{0,4},{4,8},{8,12},{12,16},{16,20},{20,24},{24,28},{1,5},{5,9},{9,... | collective-permute-start | bytes 98312 | tf_op jit(solution)/shard_map/ppermute | solution.py:18
  38.3 72.7 %collective-permute-start.9 = (f32[32,1,256]{2,1,0:T(1,128)S(1)}, f32[32,1,256]{2,1,0:T(1,128)S(1)}, u32[]{:S(2)}, u32[]{:S(2)}) collective-permute-start(f32[32,1,256]{2,1,0:T(1,128)S(1)} %slice.277), channel_id=1, source_target_pairs={{0,1},{1,2},{2,3},{4,5},{5,6},{6,7},{8,9},{9,10},{10,11},{12,13},{... | collective-permute-start | bytes 98312 | tf_op jit(solution)/shard_map/ppermute | solution.py:18
  40.5 68.0 %collective-permute-start.6 = (f32[1,32,256]{2,1,0:T(8,128)S(1)}, f32[1,32,256]{2,1,0:T(8,128)S(1)}, u32[]{:S(2)}, u32[]{:S(2)}) collective-permute-start(f32[1,32,256]{2,1,0:T(8,128)S(1)} %slice_bitcast_fusion.6), channel_id=1, source_target_pairs={{0,4},{4,8},{8,12},{12,16},{16,20},{20,24},{24,28},{1,5},{5,9},{9,... | collective-permute-start | bytes 98312 | tf_op jit(solution)/shard_map/ppermute | solution.py:18
  56.7 230.8 %copy-start.2 = (f32[32,32,257]{2,1,0:T(8,128)}, f32[32,32,257]{2,1,0:T(8,128)S(1)}, u32[]{:S(2)}) copy-start(f32[32,32,257]{2,1,0:T(8,128)S(1)} %pad.18) | copy-start | bytes 3158020
  62.0 267.6 %copy-start.3 = (f32[32,33,256]{2,1,0:T(8,128)}, f32[32,33,256]{2,1,0:T(8,128)S(1)}, u32[]{:S(2)}) copy-start(f32[32,33,256]{2,1,0:T(8,128)S(1)} %pad_maximum_fusion.14) | copy-start | bytes 3244036
  281.4 25.7 %slice-start = ((s8[6291456]{0:T(1024)(128)(4,1)}), s8[4194304]{0:T(1024)(128)(4,1)S(1)}, s32[]{:S(2)}) async-start(s8[6291456]{0:T(1024)(128)(4,1)} %bitcast.40), calls=%async_computation.2 | async-start | bytes 8388608
  281.4 25.7 %slice-start.1 = ((s8[6291456]{0:T(1024)(128)(4,1)}), s8[2097152]{0:T(1024)(128)(4,1)S(1)}, s32[]{:S(2)}) async-start(s8[6291456]{0:T(1024)(128)(4,1)} %bitcast.40), calls=%async_computation.3 | async-start | bytes 4194304
  281.4 24.9 %collective-permute-start.2 = (f32[6,1,32,256]{3,0,2,1:T(8,128)S(1)}, f32[6,1,32,256]{3,0,2,1:T(8,128)S(1)}, u32[]{:S(2)}, u32[]{:S(2)}) collective-permute-start(f32[6,1,32,256]{3,0,2,1:T(8,128)S(1)} %get-tuple-element.20), channel_id=1, source_target_pairs={{0,4},{4,8},{8,12},{12,16},{16,20},{20,24},{24,28},{1,5},{5,9},{9,... | collective-permute-start | bytes 589832 | tf_op jit(solution)/shard_map/ppermute | solution.py:26
  294.5 29.2 %copy-start.5 = (f32[33,32,256]{2,1,0:T(8,128)S(1)}, f32[33,32,256]{2,1,0:T(8,128)}, u32[]{:S(2)}) copy-start(f32[33,32,256]{2,1,0:T(8,128)} %pad_maximum_fusion.16) | copy-start | bytes 3244036
  294.5 21.2 %collective-permute-start.1 = (f32[6,1,32,256]{3,0,2,1:T(8,128)S(1)}, f32[6,1,32,256]{3,0,2,1:T(8,128)S(1)}, u32[]{:S(2)}, u32[]{:S(2)}) collective-permute-start(f32[6,1,32,256]{3,0,2,1:T(8,128)S(1)} %get-tuple-element.19), channel_id=1, source_target_pairs={{4,0},{8,4},{12,8},{16,12},{20,16},{24,20},{28,24},{5,1},{9,5},{13... | collective-permute-start | bytes 589832 | tf_op jit(solution)/shard_map/ppermute | solution.py:29
  317.6 10.8 %collective-permute-start.5 = (f32[6,34,1,256]{3,0,2,1:T(8,128)S(1)}, f32[6,34,1,256]{3,0,2,1:T(8,128)S(1)}, u32[]{:S(2)}, u32[]{:S(2)}) collective-permute-start(f32[6,34,1,256]{3,0,2,1:T(8,128)S(1)} %get-tuple-element.14), channel_id=1, source_target_pairs={{0,1},{1,2},{2,3},{4,5},{5,6},{6,7},{8,9},{9,10},{10,11},{12,13},{... | collective-permute-start | bytes 626696 | tf_op jit(solution)/shard_map/ppermute | solution.py:26
  321.7 7.9 %collective-permute-start.4 = (f32[6,34,1,256]{3,0,2,1:T(8,128)S(1)}, f32[6,34,1,256]{3,0,2,1:T(8,128)S(1)}, u32[]{:S(2)}, u32[]{:S(2)}) collective-permute-start(f32[6,34,1,256]{3,0,2,1:T(8,128)S(1)} %get-tuple-element.13), channel_id=1, source_target_pairs={{1,0},{2,1},{3,2},{5,4},{6,5},{7,6},{9,8},{10,9},{11,10},{13,12},{... | collective-permute-start | bytes 626696 | tf_op jit(solution)/shard_map/ppermute | solution.py:29
  328.4 12.6 %copy-start.7 = (f32[32,32,256]{2,1,0:T(8,128)S(1)}, f32[32,32,256]{2,1,0:T(8,128)}, u32[]{:S(2)}) copy-start(f32[32,32,256]{2,1,0:T(8,128)} %copy.66) | copy-start | bytes 3145732
  328.4 12.6 %copy-start.16 = (f32[6]{0:T(128)S(1)}, f32[6]{0:T(128)}, u32[]{:S(2)}) copy-start(f32[6]{0:T(128)} %param.14) | copy-start | bytes 76
  341.0 26.8 %copy-start.9 = (f32[32,32,257]{2,1,0:T(8,128)S(1)}, f32[32,32,257]{2,1,0:T(8,128)}, u32[]{:S(2)}) copy-start(f32[32,32,257]{2,1,0:T(8,128)} %pad.20) | copy-start | bytes 3158020
  361.5 12.9 %collective-permute-start.7 = (f32[6,1,32,256]{3,0,2,1:T(8,128)S(1)}, f32[6,1,32,256]{3,0,2,1:T(8,128)S(1)}, u32[]{:S(2)}, u32[]{:S(2)}) collective-permute-start(f32[6,1,32,256]{3,0,2,1:T(8,128)S(1)} %get-tuple-element.18), channel_id=1, source_target_pairs={{4,0},{8,4},{12,8},{16,12},{20,16},{24,20},{28,24},{5,1},{9,5},{13... | collective-permute-start | bytes 589832 | tf_op jit(solution)/shard_map/ppermute | solution.py:29
  363.5 11.5 %collective-permute-start.8 = (f32[6,1,32,256]{3,0,2,1:T(8,128)S(1)}, f32[6,1,32,256]{3,0,2,1:T(8,128)S(1)}, u32[]{:S(2)}, u32[]{:S(2)}) collective-permute-start(f32[6,1,32,256]{3,0,2,1:T(8,128)S(1)} %get-tuple-element.17), channel_id=1, source_target_pairs={{0,4},{4,8},{8,12},{12,16},{16,20},{20,24},{24,28},{1,5},{5,9},{9,... | collective-permute-start | bytes 589832 | tf_op jit(solution)/shard_map/ppermute | solution.py:26
  374.5 7.1 %copy-start.13 = (f32[33,32,256]{2,1,0:T(8,128)S(1)}, f32[33,32,256]{2,1,0:T(8,128)}, u32[]{:S(2)}) copy-start(f32[33,32,256]{2,1,0:T(8,128)} %pad_maximum_fusion.17) | copy-start | bytes 3244036
  375.1 11.1 %collective-permute-start.11 = (f32[6,34,1,256]{3,0,2,1:T(8,128)S(1)}, f32[6,34,1,256]{3,0,2,1:T(8,128)S(1)}, u32[]{:S(2)}, u32[]{:S(2)}) collective-permute-start(f32[6,34,1,256]{3,0,2,1:T(8,128)S(1)} %get-tuple-element.12), channel_id=1, source_target_pairs={{0,1},{1,2},{2,3},{4,5},{5,6},{6,7},{8,9},{9,10},{10,11},{12,13},{... | collective-permute-start | bytes 626696 | tf_op jit(solution)/shard_map/ppermute | solution.py:26
  379.5 8.0 %copy-start.10 = (f32[32,33,256]{2,1,0:T(8,128)S(1)}, f32[32,33,256]{2,1,0:T(8,128)}, u32[]{:S(2)}) copy-start(f32[32,33,256]{2,1,0:T(8,128)} %pad_maximum_fusion.15) | copy-start | bytes 3244036
  379.5 8.0 %collective-permute-start.10 = (f32[6,34,1,256]{3,0,2,1:T(8,128)S(1)}, f32[6,34,1,256]{3,0,2,1:T(8,128)S(1)}, u32[]{:S(2)}, u32[]{:S(2)}) collective-permute-start(f32[6,34,1,256]{3,0,2,1:T(8,128)S(1)} %get-tuple-element.11), channel_id=1, source_target_pairs={{1,0},{2,1},{3,2},{5,4},{6,5},{7,6},{9,8},{10,9},{11,10},{13,12},{... | collective-permute-start | bytes 626696 | tf_op jit(solution)/shard_map/ppermute | solution.py:29
  386.2 8.0 %copy-start.8 = (f32[32,32,256]{2,1,0:T(8,128)S(1)}, f32[32,32,256]{2,1,0:T(8,128)}, u32[]{:S(2)}) copy-start(f32[32,32,256]{2,1,0:T(8,128)} %copy.66) | copy-start | bytes 3145732
  412.6 25.9 %copy-start.1 = (f32[6,32,32,256]{3,0,2,1:T(8,128)}, f32[6,32,32,256]{3,0,2,1:T(8,128)S(1)}, u32[]{:S(2)}) copy-start(f32[6,32,32,256]{3,0,2,1:T(8,128)S(1)} %fusion.27) | copy-start | bytes 18874372
  412.7 14.2 %collective-permute-start.12 = (f32[6,1,32,256]{3,0,2,1:T(8,128)S(1)}, f32[6,1,32,256]{3,0,2,1:T(8,128)S(1)}, u32[]{:S(2)}, u32[]{:S(2)}) collective-permute-start(f32[6,1,32,256]{3,0,2,1:T(8,128)S(1)} %get-tuple-element.16), channel_id=1, source_target_pairs={{4,0},{8,4},{12,8},{16,12},{20,16},{24,20},{28,24},{5,1},{9,5},{13... | collective-permute-start | bytes 589832 | tf_op jit(solution)/shard_map/ppermute | solution.py:29
  414.8 12.0 %collective-permute-start.13 = (f32[6,1,32,256]{3,0,2,1:T(8,128)S(1)}, f32[6,1,32,256]{3,0,2,1:T(8,128)S(1)}, u32[]{:S(2)}, u32[]{:S(2)}) collective-permute-start(f32[6,1,32,256]{3,0,2,1:T(8,128)S(1)} %get-tuple-element.15), channel_id=1, source_target_pairs={{0,4},{4,8},{8,12},{12,16},{16,20},{20,24},{24,28},{1,5},{5,9},{9,... | collective-permute-start | bytes 589832 | tf_op jit(solution)/shard_map/ppermute | solution.py:26
  426.9 5.7 %copy-start.6 = (f32[33,32,256]{2,1,0:T(8,128)S(1)}, f32[33,32,256]{2,1,0:T(8,128)}, u32[]{:S(2)}) copy-start(f32[33,32,256]{2,1,0:T(8,128)} %pad_maximum_fusion.16) | copy-start | bytes 3244036
  426.9 10.1 %collective-permute-start.15 = (f32[6,34,1,256]{3,0,2,1:T(8,128)S(1)}, f32[6,34,1,256]{3,0,2,1:T(8,128)S(1)}, u32[]{:S(2)}, u32[]{:S(2)}) collective-permute-start(f32[6,34,1,256]{3,0,2,1:T(8,128)S(1)} %get-tuple-element.10), channel_id=1, source_target_pairs={{0,1},{1,2},{2,3},{4,5},{5,6},{6,7},{8,9},{9,10},{10,11},{12,13},{... | collective-permute-start | bytes 626696 | tf_op jit(solution)/shard_map/ppermute | solution.py:26
  430.5 8.0 %copy-start.4 = (f32[32,33,256]{2,1,0:T(8,128)S(1)}, f32[32,33,256]{2,1,0:T(8,128)}, u32[]{:S(2)}) copy-start(f32[32,33,256]{2,1,0:T(8,128)} %copy-done.3) | copy-start | bytes 3244036
  430.5 8.0 %collective-permute-start.14 = (f32[6,34,1,256]{3,0,2,1:T(8,128)S(1)}, f32[6,34,1,256]{3,0,2,1:T(8,128)S(1)}, u32[]{:S(2)}, u32[]{:S(2)}) collective-permute-start(f32[6,34,1,256]{3,0,2,1:T(8,128)S(1)} %get-tuple-element.9), channel_id=1, source_target_pairs={{1,0},{2,1},{3,2},{5,4},{6,5},{7,6},{9,8},{10,9},{11,10},{13,12},{... | collective-permute-start | bytes 626696 | tf_op jit(solution)/shard_map/ppermute | solution.py:29
where the time goes:
time: 490 us; the launch traced here: 482 us
  local copies, waits for them, and re-layouts  168 us (34%)
  other arithmetic  119 us (24%)
  waiting for transfers between devices  95.2 us (19%)
  starting transfers between devices  70.3 us (14%)
  matrix products  28.4 us (6%)
    reshape x2, local copies, waits for them, and re-layouts, assemble(): placed.reshape(BPX, BPY, BPZ, fields, BE, BE, BE)  74.8 us
    ppermute x4, waiting for transfers between devices, passed_along(): return lax.ppermute(value, axis, pairs)  44.3 us
    all_to_all x1, waiting for transfers between devices, on_device(): lax.all_to_all(outgoing, 'wide', split_axis=0, concat_axis=0, tiled=True)  43.7 us
    reshape x2, local copies, waits for them, and re-layouts, assemble(): return shaped.reshape(fields, BPX * BE, BPY * BE, BPZ * BE)  43 us
    dot_general x1, matrix products, third_section(): jnp.einsum('cj,jxyz->cxyz', coupling, center, precision=lax.Precision.HIG...  28.4 us
    ppermute x6, starting transfers between devices, padded_2(): lax.ppermute(lax.slice_in_dim(block, block.shape[dim] - width, None, axis...  26.8 us
    add x1, other arithmetic, first_section(): center + viscous_rate * diffuse(padded, geometry[0], geometry[1], geometr...  20.5 us
    ppermute x6, starting transfers between devices, padded_2(): lax.ppermute(lax.slice_in_dim(block, 0, width, axis=dim), axis, backward)  19.3 us
  transfers between devices with their start and end apart: 18, of which 7 were waited for; matrix products, arithmetic and copies ran while one was open for 17% of the time, Pallas kernels for 0%

commit v1 on v0

v1 whole, which is shorter than its diff:
```python
import functools

import jax
import jax.numpy as jnp
from jax import lax
from jax.experimental import pallas as pl
from jax.experimental.pallas import tpu as pltpu
from jax.sharding import PartitionSpec as P

BE = 16
BPX = 2
BPY = 2
BPZ = 16
COMP = 6
ADVECT = 0.2
W = 3
LX = BPX * BE
LY = BPY * BE
LZ = BPZ * BE
PX = LX + 2 * W
PY = LY + 8
CHUNKS = ((0, 3), (3, 3))
ANY = pl.BlockSpec(memory_space=pl.ANY)
SMEM = pl.BlockSpec(memory_space=pltpu.SMEM)
VMEM_LIMIT = 60 * 1024 * 1024


def pack_kernel(first, count, wide, layer, tgt, fields, out, ids, buf, tally, sem_in, sem_out):
    blocks = tgt.shape[0]
    per_peer = blocks // wide

    @pl.loop(0, wide)
    def _(d):
        tally[d] = 0

    @pl.loop(0, blocks)
    def _(b):
        t = tgt[b]
        bx = t // layer
        rest = t - bx * layer
        by = rest // BPZ
        bz = rest - by * BPZ
        dest = bx // BPX
        rank = tally[dest]
        tally[dest] = rank + 1
        place = dest * per_peer + rank
        ids[place] = ((bx - dest * BPX) * BPY + by % BPY) * BPZ + bz
        pltpu.make_async_copy(fields.at[b, pl.ds(first, count)], buf.at[place], sem_in).start()

    pltpu.make_async_copy(out, buf, sem_in).wait()
    copy = pltpu.make_async_copy(buf, out, sem_out)
    copy.start()
    copy.wait()


def pack(old_target, old_fields, first, count, wide, layer):
    blocks = old_fields.shape[0]
    shape = (blocks, count, BE, BE * BE)
    return pl.pallas_call(
        functools.partial(pack_kernel, first, count, wide, layer),
        out_shape=(
            jax.ShapeDtypeStruct(shape, jnp.float32),
            jax.ShapeDtypeStruct((blocks,), jnp.int32),
        ),
        in_specs=[SMEM, ANY],
        out_specs=(ANY, SMEM),
        scratch_shapes=[
            pltpu.VMEM(shape, jnp.float32),
            pltpu.SMEM((wide,), jnp.int32),
            pltpu.SemaphoreType.DMA,
            pltpu.SemaphoreType.DMA,
        ],
        compiler_params=pltpu.CompilerParams(vmem_limit_bytes=VMEM_LIMIT),
        cost_estimate=pl.CostEstimate(flops=0, bytes_accessed=8 * count * 16 * 256 * 64, transcendentals=0),
        name=f"pack{first}",
    )(old_target, old_fields)


def swap_groups(x):
    row = lax.broadcasted_iota(jnp.int32, x.shape, 0)
    group = lax.broadcasted_iota(jnp.int32, x.shape, 1) // BE

    def skew(x):
        for bit in (1, 2, 4):
            x = jnp.where((row & bit) != 0, pltpu.roll(x, 128 - BE * bit, 1), x)
        return x

    x = skew(x)
    for bit in (1, 2, 4):
        x = jnp.where((group & bit) != 0, pltpu.roll(x, bit, 0), x)
    return skew(x)


def unpack_kernel(count, ids, recv, v, face_lo, face_hi, stage, out, sem_in, sem_out):
    blocks = recv.shape[0]
    rows = count * BE

    @pl.loop(0, blocks)
    def _(b):
        slot = ids[b]
        bz = slot % BPZ
        place = slot - bz + (bz // 8) * 8 + (8 - bz % 8) % 8
        for half in range(2):
            pltpu.make_async_copy(
                recv.at[b, :, pl.ds(half * 128, 128)],
                stage.at[half, pl.ds(place * rows, rows)],
                sem_in,
            ).start()

    pltpu.make_async_copy(stage, stage, sem_in).wait()
    for bx in range(BPX):
        for by in range(BPY):
            base = (bx * BPY + by) * BPZ * rows

            @pl.loop(0, BE)
            def _(i):
                for c in range(count):
                    for half in range(2):
                        for top in range(2):
                            start = base + c * BE + i + top * 8 * rows
                            x = stage[half, pl.ds(start, 8, stride=rows), :]
                            out[
                                c, bx * BE + i, pl.ds(by * BE + half * 8, 8), pl.ds(top * 128, 128)
                            ] = swap_groups(x)

    copies = [
        pltpu.make_async_copy(out, v, sem_out.at[0]),
        pltpu.make_async_copy(out.at[:, pl.ds(0, W)], face_lo, sem_out.at[1]),
        pltpu.make_async_copy(out.at[:, pl.ds(LX - W, W)], face_hi, sem_out.at[2]),
    ]
    for copy in copies:
        copy.start()
    for copy in copies:
        copy.wait()


def unpack(ids, recv):
    blocks, count = recv.shape[:2]
    rows = count * BE
    face = jax.ShapeDtypeStruct((count, W, LY, LZ), jnp.float32)
    return pl.pallas_call(
        functools.partial(unpack_kernel, count),
        out_shape=(jax.ShapeDtypeStruct((count, LX, LY, LZ), jnp.float32), face, face),
        in_specs=[SMEM, ANY],
        out_specs=(ANY, ANY, ANY),
        scratch_shapes=[
            pltpu.VMEM((2, blocks * rows, 128), jnp.float32),
            pltpu.VMEM((count, LX, LY, LZ), jnp.float32),
            pltpu.SemaphoreType.DMA,
            pltpu.SemaphoreType.DMA((3,)),
        ],
        compiler_params=pltpu.CompilerParams(vmem_limit_bytes=VMEM_LIMIT),
        cost_estimate=pl.CostEstimate(flops=0, bytes_accessed=20 * count * LX * LY * LZ, transcendentals=0),
        name="unpack",
    )(ids, recv.reshape(blocks, rows, BE * BE))


def sections_kernel(first, count, has_prior, visc, coup, v, xlo, xhi, ylo, yhi, geo, *refs):
    if has_prior:
        prior, out, vb, a1, gb, tlo, thi, rb, sems = refs
    else:
        out, vb, a1, gb, tlo, thi, rb, sems = refs
    loads = [
        pltpu.make_async_copy(v, vb.at[:, pl.ds(W, LX), pl.ds(0, LY)], sems.at[0]),
        pltpu.make_async_copy(xlo, vb.at[:, pl.ds(0, W), pl.ds(0, LY)], sems.at[1]),
        pltpu.make_async_copy(xhi, vb.at[:, pl.ds(W + LX, W), pl.ds(0, LY)], sems.at[2]),
        pltpu.make_async_copy(ylo, tlo, sems.at[3]),
        pltpu.make_async_copy(yhi, thi, sems.at[4]),
        pltpu.make_async_copy(geo, gb, sems.at[5]),
    ]
    if has_prior:
        loads.append(pltpu.make_async_copy(prior, rb, sems.at[6]))
    for copy in loads:
        copy.start()
    for copy in loads:
        copy.wait()

    lane = lax.broadcasted_iota(jnp.int32, (PY, LZ), 1)
    top, bottom = lane == LZ - 1, lane == 0
    sub = lax.broadcasted_iota(jnp.int32, (8, LZ), 0)

    @pl.loop(0, PX)
    def _(x):
        for f in range(count):
            vb[f, x, pl.ds(LY, 8)] = jnp.where(sub < 4, thi[f, x], tlo[f, x])

    def up_y(a):
        return pltpu.roll(a, PY - 1, 0)

    def down_y(a):
        return pltpu.roll(a, 1, 0)

    def up_z(a):
        return jnp.where(top, 0.0, pltpu.roll(a, LZ - 1, 1))

    def down_z(a):
        return jnp.where(bottom, 0.0, pltpu.roll(a, 1, 1))

    def diffuse(src, f, x):
        c = src[f, x]
        flux = gb[0, x] * (src[f, x + 1] - c) - gb[0, x - 1] * (c - src[f, x - 1])
        flux_y = gb[1, x] * (up_y(c) - c)
        flux_z = gb[2, x] * (up_z(c) - c)
        return c, flux + (flux_y - down_y(flux_y)) + (flux_z - down_z(flux_z))

    def advect(src, f, x):
        c = src[f, x]
        flux = gb[3, x] * (src[f, x + 1] + c) - gb[3, x - 1] * (c + src[f, x - 1])
        flux_y = gb[4, x] * (up_y(c) + c)
        flux_z = gb[5, x] * (up_z(c) + c)
        return c, flux + (flux_y - down_y(flux_y)) + (flux_z - down_z(flux_z))

    @pl.loop(1, PX - 1)
    def _(x):
        for f in range(count):
            c, d = diffuse(vb, f, x)
            a1[f, x] = c + visc[first + f] * (gb[6, x] * d)

    @pl.loop(2, PX - 2)
    def _(x):
        for f in range(count):
            c, d = advect(a1, f, x)
            vb[f, x] = c - gb[6, x] * d

    @pl.loop(W, W + LX)
    def _(x):
        two = []
        own = []
        for f in range(count):
            c, d = diffuse(vb, f, x)
            own.append((c + visc[first + f] * (gb[6, x] * d))[:LY])
            two.append(c[:LY])
        for c in range(COMP):
            total = rb[c, x - W] if has_prior else None
            if first <= c < first + count:
                total = own[c - first] if total is None else total + own[c - first]
            for f in range(count):
                term = coup[c, first + f] * two[f]
                total = term if total is None else total + term
            rb[c, x - W] = total

    store = pltpu.make_async_copy(rb, out, sems.at[7])
    store.start()
    store.wait()


def sections(first, count, visc, coup, v, halos, geo, prior):
    operands = [visc, coup, v, *halos, geo]
    if prior is not None:
        operands.append(prior)
    cells = LX * LY * LZ
    return pl.pallas_call(
        functools.partial(sections_kernel, first, count, prior is not None),
        out_shape=jax.ShapeDtypeStruct((COMP, LX, LY, LZ), jnp.float32),
        in_specs=[SMEM, SMEM] + [ANY] * (len(operands) - 2),
        out_specs=ANY,
        scratch_shapes=[
            pltpu.VMEM((count, PX, PY, LZ), jnp.float32),
            pltpu.VMEM((count, PX, PY, LZ), jnp.float32),
            pltpu.VMEM((7, PX, PY, LZ), jnp.float32),
            pltpu.VMEM((count, PX, 8, LZ), jnp.float32),
            pltpu.VMEM((count, PX, 8, LZ), jnp.float32),
            pltpu.VMEM((COMP, LX, LY, LZ), jnp.float32),
            pltpu.SemaphoreType.DMA((8,)),
        ],
        compiler_params=pltpu.CompilerParams(vmem_limit_bytes=VMEM_LIMIT),
        cost_estimate=pl.CostEstimate(
            flops=cells * count * 80, bytes_accessed=4 * cells * (count + 20), transcendentals=0
        ),
        name=f"sections{first}",
    )(*operands)


def forward(value, axis):
    count = lax.axis_size(axis)
    return lax.ppermute(value, axis, [(i, i + 1) for i in range(count - 1)])


def backward(value, axis):
    count = lax.axis_size(axis)
    return lax.ppermute(value, axis, [(i + 1, i) for i in range(count - 1)])


def y_halos(xlo, center, xhi):
    rows = jnp.concatenate([a[:, :, LY - 8 :] for a in (xlo, center, xhi)], 1)
    low = forward(rows, "narrow")
    rows = jnp.concatenate([a[:, :, :8] for a in (xlo, center, xhi)], 1)
    return low, backward(rows, "narrow")


BELOW = ((0, 3), (0, 2), (0, 1), (1, 2), (1, 1), (2, 2), (2, 1), (6, 2), (6, 1), (3, 2), (3, 1), (4, 1), (5, 1))
ABOVE = ((0, 1), (0, 2), (1, 1), (1, 2), (2, 1), (2, 2), (6, 1), (6, 2), (3, 1), (4, 1), (5, 1))


def geometry(cut_flag, apertures, volume, velocity):
    cut_cells = jnp.repeat(jnp.repeat(jnp.repeat(cut_flag, BE, 0), BE, 1), BE, 2) > 0
    face_open = jnp.where(cut_cells[None], apertures, 1.0)
    inverse = 1.0 / jnp.where(cut_cells, volume, 1.0)
    transport = face_open * velocity * (0.5 * ADVECT)
    center = jnp.concatenate([face_open, transport, inverse[None]], 0)
    low = forward(jnp.stack([center[a, LX - d] for a, d in BELOW]), "wide")
    high = backward(jnp.stack([center[a, d - 1] for a, d in ABOVE]), "wide")
    zero = jnp.zeros((LY, LZ), jnp.float32)
    below = {key: low[n] for n, key in enumerate(BELOW)}
    above = {key: high[n] for n, key in enumerate(ABOVE)}
    xlo = jnp.stack([jnp.stack([below.get((a, d), zero) for d in (3, 2, 1)]) for a in range(7)])
    xhi = jnp.stack([jnp.stack([above.get((a, d), zero) for d in (1, 2, 3)]) for a in range(7)])
    ylo, yhi = y_halos(xlo, center, xhi)
    rows = jnp.concatenate([xlo, center, xhi], 1)
    edge = jnp.where(jnp.arange(8)[:, None] < 4, yhi, ylo)
    return jnp.concatenate([rows, edge], 2)


def on_device(old_fields, old_target, cut_flag, apertures, volume, velocity, diffusivity, coupling):
    wide = lax.axis_size("wide")
    layer = BPY * lax.axis_size("narrow") * BPZ
    received = []
    for first, count in CHUNKS:
        outgoing, ids = pack(old_target, old_fields, first, count, wide, layer)
        received.append(lax.all_to_all(outgoing, "wide", 0, 0, tiled=True))
        if first == 0:
            slots = lax.all_to_all(ids, "wide", 0, 0, tiled=True)
    geo = geometry(cut_flag, apertures, volume, velocity)
    result = None
    for (first, count), recv in zip(CHUNKS, received):
        v, face_lo, face_hi = unpack(slots, recv)
        xlo, xhi = forward(face_hi, "wide"), backward(face_lo, "wide")
        ylo, yhi = y_halos(xlo, v, xhi)
        result = sections(
            first, count, diffusivity, coupling, v, (xlo, xhi, ylo, yhi), geo, result
        )
    return result


def solution(mesh):
    in_specs = (
        P(("wide", "narrow"), None, None, None),
        P(("wide", "narrow")),
        P("wide", "narrow", None),
        P(None, "wide", "narrow", None),
        P("wide", "narrow", None),
        P(None, "wide", "narrow", None),
        P(),
        P(),
    )
    out_specs = P(None, "wide", "narrow", None)
    return jax.shard_map(
        on_device, mesh=mesh, in_specs=in_specs, out_specs=out_specs, check_vma=False
    )
```

time: 490 us -> 361 us (0.74); the launches traced: 482 us -> 360 us
  local copies, waits for them, and re-layouts: 168 us -> 25.7 us
  Pallas kernels: 0 us -> 140 us
  other arithmetic: 119 us -> 20.5 us
  matrix products: 28.4 us -> 0 us
  blocking collectives: 0 us -> 7.69 us
    pallas_call x0 -> x6, Pallas kernels: none -> 140 us  [the longest x2 66.2 us: unpack(): pl.pallas_call(functools.partial(unpack_kernel, count), out_shape=(jax.Sh...]
    reshape x4 -> x0, local copies, waits for them, and re-layouts: 118 us -> none  [the longest x2 74.8 us: assemble(): placed.reshape(BPX, BPY, BPZ, fields, BE, BE, BE)]
    mul x10 -> x1, other arithmetic: 63.4 us -> 5.74 us  [geometry(): transport = face_open * velocity * (0.5 * ADVECT)]
    dot_general x1 -> x0, matrix products: 28.4 us -> none  [third_section(): jnp.einsum('cj,jxyz->cxyz', coupling, center, precision=lax.Precision.HIG...]
    add x2 -> x0, other arithmetic: 21.2 us -> none  [the longest x1 20.5 us: first_section(): center + viscous_rate * diffuse(padded, geometry[0], geometry[1], geometr...]
    sub x1 -> x0, other arithmetic: 18.4 us -> none  [second_section(): center - ADVECT * advect(padded, geometry[3], geometry[4], geometry[5]) /...]
    gather x3 -> x0, local copies, waits for them, and re-layouts: 14.3 us -> none  [the longest x1 6.44 us: on_device(): adjoint = assemble(arrived[invert])]
    add x1 -> x0, local copies, waits for them, and re-layouts: 8.11 us -> none  [third_section(): center + viscous_rate * diffuse(padded, geometry[0], geometry[1], geometr...]
  transfers between devices with their start and end apart: 18 -> 14, of which waited for: 7 -> 3; matrix products, arithmetic and copies ran while one was open for 17% -> 12% of each run, Pallas kernels for 0% -> 28%
where the time goes in v1:
time: 361 us; the launch traced here: 360 us
  Pallas kernels  140 us (39%)
  waiting for transfers between devices  95.7 us (27%)
  starting transfers between devices  69.8 us (19%)
  local copies, waits for them, and re-layouts  25.7 us (7%)
  other arithmetic  20.5 us (6%)
  blocking collectives  7.69 us (2%)
    pallas_call x2, Pallas kernels, unpack(): pl.pallas_call(functools.partial(unpack_kernel, count), out_shape=(jax.Sh...  66.2 us
    pallas_call x2, Pallas kernels, sections(): pl.pallas_call(functools.partial(sections_kernel, first, count, prior is...  62 us
    all_to_all x2, waiting for transfers between devices, on_device(): received.append(lax.all_to_all(outgoing, 'wide', 0, 0, tiled=True))  48.7 us
    ppermute x6, waiting for transfers between devices, backward(): return lax.ppermute(value, axis, [(i + 1, i) for i in range(count - 1)])  43.7 us
    ppermute x6, starting transfers between devices, backward(): return lax.ppermute(value, axis, [(i + 1, i) for i in range(count - 1)])  35.8 us
    ppermute x6, starting transfers between devices, forward(): return lax.ppermute(value, axis, [(i, i + 1) for i in range(count - 1)])  19.2 us
    all_to_all x2, starting transfers between devices, on_device(): received.append(lax.all_to_all(outgoing, 'wide', 0, 0, tiled=True))  14.9 us
    unnamed x59, local copies, waits for them, and re-layouts  14 us
  transfers between devices with their start and end apart: 14, of which 3 were waited for; matrix products, arithmetic and copies ran while one was open for 12% of the time, Pallas kernels for 28%

profile of v1, /device:TPU:21, one launch (start us, length us, event | category | flops | bytes accessed | tf_op | source)
XLA Modules:
  0.0 359.7 jit_solution(7063629900741450580)
XLA Ops:
  0.0 5.7 %pack0.1 = (f32[64,3,16,256]{3,2,1,0:T(8,128)}, s32[64]{0:T(128)}) custom-call(s32[64]{0:T(128)} %tgt.3, f32[64,6,16,256]{3,2,1,0:T(8,128)} %fields.3), custom_call_target="tpu_custom_call" | custom-call | bytes 6291456 | tf_op jit(solution)/shard_map/pack0/pallas_call | solution.py:59
  5.8 0.7 all_to_all.13
  6.5 7.7 %all_to_all.21 = s32[8,8,1]{1,2,0:T(1,128)S(1)} all-to-all(s32[8,8,1]{1,2,0:T(1,128)S(1)} %bitcast.140), channel_id=1, replica_groups=mesh['wide'=8,'narrow'=4] {'wide'}, dimensions={0} | all-to-all | bytes 512 | tf_op jit(solution)/shard_map/all_to_all | solution.py:322
  14.2 7.4 %all-to-all-start.2 = ((f32[64,3,16,256]{3,2,1,0:T(8,128)}), f32[64,3,16,256]{3,2,1,0:T(8,128)}, u32[]{:S(2)}, u32[]{:S(2)}) async-start(f32[64,3,16,256]{3,2,1,0:T(8,128)} %get-tuple-element.19), calls=%async_computation.2 | async-start | bytes 6291456 | tf_op jit(solution)/shard_map/all_to_all | solution.py:320
  21.6 5.8 %pack3.1 = (f32[64,3,16,256]{3,2,1,0:T(8,128)}, s32[64]{0:T(128)}) custom-call(s32[64]{0:T(128)} %tgt.3, f32[64,6,16,256]{3,2,1,0:T(8,128)} %fields.3), custom_call_target="tpu_custom_call" | custom-call | bytes 6291456 | tf_op jit(solution)/shard_map/pack3/pallas_call | solution.py:59
  27.4 0.1 copy.23
  27.5 0.2 copy.24
  27.8 0.3 broadcast_in_dim.38
  28.1 1.4 copy.25
  29.5 0.0 copy-start.10
  29.5 5.7 %multiply_multiply_fusion = (f32[3,32,32,256]{3,2,1,0:T(8,128)}, f32[3,32,32,256]{3,2,1,0:T(8,128)S(1)}) fusion(f32[3,32,32,256]{3,2,1,0:T(8,128)} %param.13, f32[3,32,32,256]{3,2,1,0:T(8,128)} %param.11, pred[32,32,256]{2,1,0:T(8,128)(4,1)S(1)} %copy.25), kind=kLoop, calls=%fused_computation.1 | loop fusion | flops 2359296 | bytes 12845056 | tf_op jit(solution)/shard_map/mul | solution.py:299
  35.3 0.6 constant_dynamic-update-slice_fusion.12
  35.9 0.6 constant_dynamic-update-slice_fusion.11
  36.5 0.6 constant_dynamic-update-slice_fusion.10
  37.1 0.6 constant_dynamic-update-slice_fusion.9
  37.7 0.6 constant_dynamic-update-slice_fusion.8
  38.3 0.6 constant_dynamic-update-slice_fusion.7
  39.0 1.1 divide_bitcast_fusion
  40.1 48.7 %all-to-all-done.2 = f32[64,3,16,256]{3,2,1,0:T(8,128)} async-done(((f32[64,3,16,256]{3,2,1,0:T(8,128)}), f32[64,3,16,256]{3,2,1,0:T(8,128)}, u32[]{:S(2)}, u32[]{:S(2)}) %all-to-all-start.2) | async-done | bytes 3145760 | tf_op jit(solution)/shard_map/all_to_all | solution.py:320
  88.8 7.5 %all-to-all-start.1 = ((f32[64,3,16,256]{3,2,1,0:T(8,128)}), f32[64,3,16,256]{3,2,1,0:T(8,128)}, u32[]{:S(2)}, u32[]{:S(2)}) async-start(f32[64,3,16,256]{3,2,1,0:T(8,128)} %get-tuple-element.15), calls=%async_computation.1 | async-start | bytes 6291456 | tf_op jit(solution)/shard_map/all_to_all | solution.py:320
  96.3 0.6 constant_dynamic-update-slice_fusion.6
  96.9 1.7 constant_dynamic-update-slice_fusion.5
  98.6 1.4 constant_dynamic-update-slice_fusion.4
  100.0 1.4 constant_dynamic-update-slice_fusion.3
  101.4 1.4 constant_dynamic-update-slice_fusion.2
  102.8 1.4 constant_dynamic-update-slice_fusion.1
  104.2 1.4 constant_dynamic-update-slice_fusion
  105.6 2.2 collective-permute-start.5
  107.8 4.0 %collective-permute-start.4 = (f32[13,32,256]{2,1,0:T(8,128)}, f32[13,32,256]{2,1,0:T(8,128)S(1)}, u32[]{:S(2)}, u32[]{:S(2)}) collective-permute-start(f32[13,32,256]{2,1,0:T(8,128)} %get-tuple-element.29), channel_id=1, source_target_pairs={{0,4},{4,8},{8,12},{12,16},{16,20},{20,24},{24,28},{1,5},{5,9},{9,... | collective-permute-start | bytes 1277960 | tf_op jit(solution)/shard_map/ppermute | solution.py:276
  111.8 43.7 %collective-permute-done.5 = f32[11,32,256]{2,1,0:T(8,128)S(1)} collective-permute-done((f32[11,32,256]{2,1,0:T(8,128)}, f32[11,32,256]{2,1,0:T(8,128)S(1)}, u32[]{:S(2)}, u32[]{:S(2)}) %collective-permute-start.5) | collective-permute-done | bytes 360480 | tf_op jit(solution)/shard_map/ppermute | solution.py:281
  155.4 0.1 fusion.5
  155.8 0.7 copy-done.6
  156.5 0.1 fusion.9
  156.6 0.8 copy-done.8
  157.4 2.4 fusion.1
  159.7 4.2 %collective-permute-start.6 = (f32[7,38,8,256]{3,2,1,0:T(8,128)}, f32[7,38,8,256]{3,2,1,0:T(8,128)}, u32[]{:S(2)}, u32[]{:S(2)}) collective-permute-start(f32[7,38,8,256]{3,2,1,0:T(8,128)} %get-tuple-element.26), channel_id=1, source_target_pairs={{1,0},{2,1},{3,2},{5,4},{6,5},{7,6},{9,8},{10,9},{11,10},{13,12},{... | collective-permute-start | bytes 6537224 | tf_op jit(solution)/shard_map/ppermute | solution.py:281
  164.0 3.0 collective-permute-start.7
  167.0 0.5 broadcast.66
  167.5 0.7 reduce.3
  168.2 0.6 all_to_all.15.ids
  168.8 33.1 %unpack.3 = (f32[3,32,32,256]{3,2,1,0:T(8,128)}, f32[3,3,32,256]{3,2,1,0:T(8,128)}, f32[3,3,32,256]{3,2,1,0:T(8,128)}) custom-call(s32[64]{0:T(128)} %all_to_all.15.ids, f32[64,48,256]{2,1,0:T(8,128)} %bitcast.44.recv), custom_call_target="tpu_custom_call" | custom-call | bytes 15728640 | tf_op jit(solution)/shard_map/unpack/pallas_call | solution.py:141
  201.9 1.9 collective-permute-start.8
  203.8 2.7 fusion.7
  206.5 19.6 %collective-permute-start.9 = (f32[3,3,32,256]{3,2,1,0:T(8,128)}, f32[3,3,32,256]{3,2,1,0:T(8,128)}, u32[]{:S(2)}, u32[]{:S(2)}) collective-permute-start(f32[3,3,32,256]{3,2,1,0:T(8,128)} %get-tuple-element.22), channel_id=1, source_target_pairs={{4,0},{8,4},{12,8},{16,12},{20,16},{24,20},{28,24},{5,1},{9,5},{13... | collective-permute-start | bytes 884744 | tf_op jit(solution)/shard_map/ppermute | solution.py:281
  226.2 33.1 %unpack.2 = (f32[3,32,32,256]{3,2,1,0:T(8,128)}, f32[3,3,32,256]{3,2,1,0:T(8,128)}, f32[3,3,32,256]{3,2,1,0:T(8,128)}) custom-call(s32[64]{0:T(128)} %all_to_all.15.ids, f32[64,48,256]{2,1,0:T(8,128)} %bitcast.1.recv), custom_call_target="tpu_custom_call" | custom-call | bytes 15728640 | tf_op jit(solution)/shard_map/unpack/pallas_call | solution.py:141
  259.3 1.6 fusion.8
  260.9 1.9 collective-permute-start
  262.9 0.7 copy-done.13
  263.6 4.2 %collective-permute-start.1 = (f32[3,3,32,256]{3,2,1,0:T(8,128)S(1)}, f32[3,3,32,256]{3,2,1,0:T(8,128)S(1)}, u32[]{:S(2)}, u32[]{:S(2)}) collective-permute-start(f32[3,3,32,256]{3,2,1,0:T(8,128)S(1)} %copy-done.16), channel_id=1, source_target_pairs={{4,0},{8,4},{12,8},{16,12},{20,16},{24,20},{28,24},{5,1},{9,5},{13... | collective-permute-start | bytes 884744 | tf_op jit(solution)/shard_map/ppermute | solution.py:281
  267.9 0.9 fusion.15
  268.8 0.9 fusion.16
  269.8 0.1 pad_maximum_fusion.7
  269.9 4.4 %collective-permute-start.10 = (f32[3,38,8,256]{3,2,1,0:T(8,128)S(1)}, f32[3,38,8,256]{3,2,1,0:T(8,128)}, u32[]{:S(2)}, u32[]{:S(2)}) collective-permute-start(f32[3,38,8,256]{3,2,1,0:T(8,128)S(1)} %pad_maximum_fusion.7), channel_id=1, source_target_pairs={{0,1},{1,2},{2,3},{4,5},{5,6},{6,7},{8,9},{9,10},{10,11},{12,13},{... | collective-permute-start | bytes 2801672 | tf_op jit(solution)/shard_map/ppermute | solution.py:276
  274.3 0.1 pad_maximum_fusion.8
  274.4 3.3 collective-permute-done.xlo
  277.7 3.6 %collective-permute-start.11 = (f32[3,38,8,256]{3,2,1,0:T(8,128)S(1)}, f32[3,38,8,256]{3,2,1,0:T(8,128)}, u32[]{:S(2)}, u32[]{:S(2)}) collective-permute-start(f32[3,38,8,256]{3,2,1,0:T(8,128)S(1)} %pad_maximum_fusion.8), channel_id=1, source_target_pairs={{1,0},{2,1},{3,2},{5,4},{6,5},{7,6},{9,8},{10,9},{11,10},{13,12},{... | collective-permute-start | bytes 2801672 | tf_op jit(solution)/shard_map/ppermute | solution.py:281
  281.4 1.0 pad_maximum_fusion.6
  282.5 1.9 collective-permute-start.3
  284.4 1.1 pad_maximum_fusion.5
  285.5 3.9 %collective-permute-start.2 = (f32[3,38,8,256]{3,2,1,0:T(8,128)}, f32[3,38,8,256]{3,2,1,0:T(8,128)}, u32[]{:S(2)}, u32[]{:S(2)}) collective-permute-start(f32[3,38,8,256]{3,2,1,0:T(8,128)} %pad_maximum_fusion.5), channel_id=1, source_target_pairs={{0,1},{1,2},{2,3},{4,5},{5,6},{6,7},{8,9},{9,10},{10,11},{12,13},{... | collective-permute-start | bytes 2801672 | tf_op jit(solution)/shard_map/ppermute | solution.py:276
  289.4 2.6 broadcast_select_fusion.1
  292.1 5.6 %pad_maximum_fusion.geo = f32[7,38,40,256]{3,2,1,0:T(8,128)} fusion(f32[7,38,8,256]{3,2,1,0:T(8,128)S(1)} %broadcast_select_fusion.1, f32[7,3,32,256]{3,2,1,0:T(8,128)S(1)} %copy-done.7, f32[1,32,32,256]{3,2,1,0:T(8,128)S(1)} %copy-done.3, f32[3,32,32,256]{3,2,1,0:T(8,128)S(1)} %copy-done.1, f32[3,32,32,256]{3,2,1,0:T(8,128)S(1)} %get-tuple-element.24, ...), kind=kLoop, calls=%fused_computation | loop fusion | flops 13619200 | bytes 21790720 | tf_op jit(solution)/shard_map/concatenate | solution.py:311
  297.7 30.0 %sections0.1.refs_0_ = f32[6,32,32,256]{3,2,1,0:T(8,128)} custom-call(f32[6]{0:T(128)} %visc.3, f32[6,6]{1,0:T(8,128)} %coup.3, f32[3,32,32,256]{3,2,1,0:T(8,128)} %get-tuple-element.20.v, f32[3,3,32,256]{3,2,1,0:T(8,128)} %copy-done.13, f32[3,3,32,256]{3,2,1,0:T(8,128)} %collective-permute-done.9.xhi, f32[3,38,8,256]{3,2,1,0:T(8,128)} %collective-permute-done.10.ylo, ...), custom_call_target="tpu_custom_call" | custom-call | flops 62914560 | bytes 24117248 | tf_op jit(solution)/shard_map/sections0/pallas_call | solution.py:252
  327.8 31.9 %sections3.1 = f32[6,32,32,256]{3,2,1,0:T(8,128)} custom-call(f32[6]{0:T(128)} %visc.3, f32[6,6]{1,0:T(8,128)} %coup.3, f32[3,32,32,256]{3,2,1,0:T(8,128)} %get-tuple-element.16.v, f32[3,3,32,256]{3,2,1,0:T(8,128)} %copy-done.11, f32[3,3,32,256]{3,2,1,0:T(8,128)} %copy-done.12, f32[3,38,8,256]{3,2,1,0:T(8,128)} %collective-permute-done.2.ylo, ...), custom_call_target="tpu_custom_call" | custom-call | flops 62914560 | bytes 24117248 | tf_op jit(solution)/shard_map/sections3/pallas_call | solution.py:252
  (67 shorter events, 0.3 us)
Async XLA Ops:
  14.2 74.6 %all-to-all-start.2 = ((f32[64,3,16,256]{3,2,1,0:T(8,128)}), f32[64,3,16,256]{3,2,1,0:T(8,128)}, u32[]{:S(2)}, u32[]{:S(2)}) async-start(f32[64,3,16,256]{3,2,1,0:T(8,128)} %get-tuple-element.19), calls=%async_computation.2 | async-start | bytes 6291456 | tf_op jit(solution)/shard_map/all_to_all | solution.py:320
  21.6 5.8 %copy-start.14 = (s32[2,2,16]{2,1,0:T(2,128)S(1)}, s32[2,2,16]{2,1,0:T(2,128)}, u32[]{:S(2)}) copy-start(s32[2,2,16]{2,1,0:T(2,128)} %param.10) | copy-start | bytes 772
  29.5 9.5 %copy-start.10 = (f32[32,32,256]{2,1,0:T(8,128)S(1)}, f32[32,32,256]{2,1,0:T(8,128)}, u32[]{:S(2)}) copy-start(f32[32,32,256]{2,1,0:T(8,128)} %param.12) | copy-start | bytes 3145732
  88.8 66.6 %copy-start.15 = (pred[3]{0:T(512)(128)(4,1)S(1)}, pred[3]{0:T(512)(128)(4,1)}, u32[]{:S(2)}) copy-start(pred[3]{0:T(512)(128)(4,1)} %constant.4.clone.1) | copy-start | bytes 13
  88.8 137.3 %all-to-all-start.1 = ((f32[64,3,16,256]{3,2,1,0:T(8,128)}), f32[64,3,16,256]{3,2,1,0:T(8,128)}, u32[]{:S(2)}, u32[]{:S(2)}) async-start(f32[64,3,16,256]{3,2,1,0:T(8,128)} %get-tuple-element.15), calls=%async_computation.1 | async-start | bytes 6291456 | tf_op jit(solution)/shard_map/all_to_all | solution.py:320
  96.3 61.1 %copy-start = (f32[3,32,32,256]{3,2,1,0:T(8,128)S(1)}, f32[3,32,32,256]{3,2,1,0:T(8,128)}, u32[]{:S(2)}) copy-start(f32[3,32,32,256]{3,2,1,0:T(8,128)} %get-tuple-element.23) | copy-start | bytes 9437188
  96.3 61.1 %copy-start.2 = (f32[1,32,32,256]{3,2,1,0:T(8,128)S(1)}, f32[1,32,32,256]{3,2,1,0:T(8,128)}, u32[]{:S(2)}) copy-start(f32[1,32,32,256]{3,2,1,0:T(8,128)} %divide_bitcast_fusion) | copy-start | bytes 3145732
  105.6 49.8 %collective-permute-start.5 = (f32[11,32,256]{2,1,0:T(8,128)}, f32[11,32,256]{2,1,0:T(8,128)S(1)}, u32[]{:S(2)}, u32[]{:S(2)}) collective-permute-start(f32[11,32,256]{2,1,0:T(8,128)} %get-tuple-element.30), channel_id=1, source_target_pairs={{4,0},{8,4},{12,8},{16,12},{20,16},{24,20},{28,24},{5,1},{9,5},{13... | collective-permute-start | bytes 1081352 | tf_op jit(solution)/shard_map/ppermute | solution.py:281
  107.8 47.9 %collective-permute-start.4 = (f32[13,32,256]{2,1,0:T(8,128)}, f32[13,32,256]{2,1,0:T(8,128)S(1)}, u32[]{:S(2)}, u32[]{:S(2)}) collective-permute-start(f32[13,32,256]{2,1,0:T(8,128)} %get-tuple-element.29), channel_id=1, source_target_pairs={{0,4},{4,8},{8,12},{12,16},{16,20},{20,24},{24,28},{1,5},{5,9},{9,... | collective-permute-start | bytes 1277960 | tf_op jit(solution)/shard_map/ppermute | solution.py:276
  155.6 0.9 copy-start.6
  156.5 0.9 copy-start.8
  159.7 125.8 %collective-permute-start.6 = (f32[7,38,8,256]{3,2,1,0:T(8,128)}, f32[7,38,8,256]{3,2,1,0:T(8,128)}, u32[]{:S(2)}, u32[]{:S(2)}) collective-permute-start(f32[7,38,8,256]{3,2,1,0:T(8,128)} %get-tuple-element.26), channel_id=1, source_target_pairs={{1,0},{2,1},{3,2},{5,4},{6,5},{7,6},{9,8},{10,9},{11,10},{13,12},{... | collective-permute-start | bytes 6537224 | tf_op jit(solution)/shard_map/ppermute | solution.py:281
  164.0 125.4 %collective-permute-start.7 = (f32[7,38,8,256]{3,2,1,0:T(8,128)}, f32[7,38,8,256]{3,2,1,0:T(8,128)}, u32[]{:S(2)}, u32[]{:S(2)}) collective-permute-start(f32[7,38,8,256]{3,2,1,0:T(8,128)} %get-tuple-element.25), channel_id=1, source_target_pairs={{0,1},{1,2},{2,3},{4,5},{5,6},{6,7},{8,9},{9,10},{10,11},{12,13},{... | collective-permute-start | bytes 6537224 | tf_op jit(solution)/shard_map/ppermute | solution.py:276
  201.9 61.0 %collective-permute-start.8 = (f32[3,3,32,256]{3,2,1,0:T(8,128)}, f32[3,3,32,256]{3,2,1,0:T(8,128)S(1)}, u32[]{:S(2)}, u32[]{:S(2)}) collective-permute-start(f32[3,3,32,256]{3,2,1,0:T(8,128)} %get-tuple-element.21), channel_id=1, source_target_pairs={{0,4},{4,8},{8,12},{12,16},{16,20},{20,24},{24,28},{1,5},{5,9},{9,... | collective-permute-start | bytes 884744 | tf_op jit(solution)/shard_map/ppermute | solution.py:276
  206.5 62.3 %collective-permute-start.9 = (f32[3,3,32,256]{3,2,1,0:T(8,128)}, f32[3,3,32,256]{3,2,1,0:T(8,128)}, u32[]{:S(2)}, u32[]{:S(2)}) collective-permute-start(f32[3,3,32,256]{3,2,1,0:T(8,128)} %get-tuple-element.22), channel_id=1, source_target_pairs={{4,0},{8,4},{12,8},{16,12},{20,16},{24,20},{28,24},{5,1},{9,5},{13... | collective-permute-start | bytes 884744 | tf_op jit(solution)/shard_map/ppermute | solution.py:281
  259.3 1.7 copy-start.17
  259.3 4.4 %copy-start.16 = (f32[3,3,32,256]{3,2,1,0:T(8,128)S(1)}, f32[3,3,32,256]{3,2,1,0:T(8,128)}, u32[]{:S(2)}) copy-start(f32[3,3,32,256]{3,2,1,0:T(8,128)} %get-tuple-element.18) | copy-start | bytes 884740
  259.3 10.5 %copy-start.5 = (f32[3,32,8,256]{3,2,1,0:T(8,128)S(1)}, f32[3,32,8,256]{3,2,1,0:T(8,128)}, u32[]{:S(2)}) copy-start(f32[3,32,8,256]{3,2,1,0:T(8,128)} %get-tuple-element.28) | copy-start | bytes 2359300
  259.3 15.0 %copy-start.4 = (f32[3,32,8,256]{3,2,1,0:T(8,128)S(1)}, f32[3,32,8,256]{3,2,1,0:T(8,128)}, u32[]{:S(2)}) copy-start(f32[3,32,8,256]{3,2,1,0:T(8,128)} %get-tuple-element.27) | copy-start | bytes 2359300
  260.9 16.8 %collective-permute-start = (f32[3,3,32,256]{3,2,1,0:T(8,128)S(1)}, f32[3,3,32,256]{3,2,1,0:T(8,128)S(1)}, u32[]{:S(2)}, u32[]{:S(2)}) collective-permute-start(f32[3,3,32,256]{3,2,1,0:T(8,128)S(1)} %copy-done.17), channel_id=1, source_target_pairs={{0,4},{4,8},{8,12},{12,16},{16,20},{20,24},{24,28},{1,5},{5,9},{9,... | collective-permute-start | bytes 884744 | tf_op jit(solution)/shard_map/ppermute | solution.py:276
  262.9 0.7 copy-start.13
  263.6 17.8 %collective-permute-start.1 = (f32[3,3,32,256]{3,2,1,0:T(8,128)S(1)}, f32[3,3,32,256]{3,2,1,0:T(8,128)S(1)}, u32[]{:S(2)}, u32[]{:S(2)}) collective-permute-start(f32[3,3,32,256]{3,2,1,0:T(8,128)S(1)} %copy-done.16), channel_id=1, source_target_pairs={{4,0},{8,4},{12,8},{16,12},{20,16},{24,20},{28,24},{5,1},{9,5},{13... | collective-permute-start | bytes 884744 | tf_op jit(solution)/shard_map/ppermute | solution.py:281
  269.9 27.8 %collective-permute-start.10 = (f32[3,38,8,256]{3,2,1,0:T(8,128)S(1)}, f32[3,38,8,256]{3,2,1,0:T(8,128)}, u32[]{:S(2)}, u32[]{:S(2)}) collective-permute-start(f32[3,38,8,256]{3,2,1,0:T(8,128)S(1)} %pad_maximum_fusion.7), channel_id=1, source_target_pairs={{0,1},{1,2},{2,3},{4,5},{5,6},{6,7},{8,9},{9,10},{10,11},{12,13},{... | collective-permute-start | bytes 2801672 | tf_op jit(solution)/shard_map/ppermute | solution.py:276
  277.7 14.3 %copy-start.11 = (f32[3,3,32,256]{3,2,1,0:T(8,128)}, f32[3,3,32,256]{3,2,1,0:T(8,128)S(1)}, u32[]{:S(2)}) copy-start(f32[3,3,32,256]{3,2,1,0:T(8,128)S(1)} %collective-permute-done.xlo) | copy-start | bytes 884740
  277.7 20.0 %collective-permute-start.11 = (f32[3,38,8,256]{3,2,1,0:T(8,128)S(1)}, f32[3,38,8,256]{3,2,1,0:T(8,128)}, u32[]{:S(2)}, u32[]{:S(2)}) collective-permute-start(f32[3,38,8,256]{3,2,1,0:T(8,128)S(1)} %pad_maximum_fusion.8), channel_id=1, source_target_pairs={{1,0},{2,1},{3,2},{5,4},{6,5},{7,6},{9,8},{10,9},{11,10},{13,12},{... | collective-permute-start | bytes 2801672 | tf_op jit(solution)/shard_map/ppermute | solution.py:281
  281.4 10.6 %copy-start.12 = (f32[3,3,32,256]{3,2,1,0:T(8,128)}, f32[3,3,32,256]{3,2,1,0:T(8,128)S(1)}, u32[]{:S(2)}) copy-start(f32[3,3,32,256]{3,2,1,0:T(8,128)S(1)} %collective-permute-done.1.xhi) | copy-start | bytes 884740
  282.5 45.3 %collective-permute-start.3 = (f32[3,38,8,256]{3,2,1,0:T(8,128)}, f32[3,38,8,256]{3,2,1,0:T(8,128)}, u32[]{:S(2)}, u32[]{:S(2)}) collective-permute-start(f32[3,38,8,256]{3,2,1,0:T(8,128)} %pad_maximum_fusion.6), channel_id=1, source_target_pairs={{1,0},{2,1},{3,2},{5,4},{6,5},{7,6},{9,8},{10,9},{11,10},{13,12},{... | collective-permute-start | bytes 2801672 | tf_op jit(solution)/shard_map/ppermute | solution.py:281
  285.5 6.6 %copy-start.1 = (f32[3,32,32,256]{3,2,1,0:T(8,128)S(1)}, f32[3,32,32,256]{3,2,1,0:T(8,128)}, u32[]{:S(2)}) copy-start(f32[3,32,32,256]{3,2,1,0:T(8,128)} %get-tuple-element.23) | copy-start | bytes 9437188
  285.5 6.6 %copy-start.3 = (f32[1,32,32,256]{3,2,1,0:T(8,128)S(1)}, f32[1,32,32,256]{3,2,1,0:T(8,128)}, u32[]{:S(2)}) copy-start(f32[1,32,32,256]{3,2,1,0:T(8,128)} %divide_bitcast_fusion) | copy-start | bytes 3145732
  285.5 6.6 %copy-start.7 = (f32[7,3,32,256]{3,2,1,0:T(8,128)S(1)}, f32[7,3,32,256]{3,2,1,0:T(8,128)}, u32[]{:S(2)}) copy-start(f32[7,3,32,256]{3,2,1,0:T(8,128)} %copy-done.6) | copy-start | bytes 2064388
  285.5 6.6 %copy-start.9 = (f32[7,3,32,256]{3,2,1,0:T(8,128)S(1)}, f32[7,3,32,256]{3,2,1,0:T(8,128)}, u32[]{:S(2)}) copy-start(f32[7,3,32,256]{3,2,1,0:T(8,128)} %copy-done.8) | copy-start | bytes 2064388
  285.5 42.3 %collective-permute-start.2 = (f32[3,38,8,256]{3,2,1,0:T(8,128)}, f32[3,38,8,256]{3,2,1,0:T(8,128)}, u32[]{:S(2)}, u32[]{:S(2)}) collective-permute-start(f32[3,38,8,256]{3,2,1,0:T(8,128)} %pad_maximum_fusion.5), channel_id=1, source_target_pairs={{0,1},{1,2},{2,3},{4,5},{5,6},{6,7},{8,9},{9,10},{10,11},{12,13},{... | collective-permute-start | bytes 2801672 | tf_op jit(solution)/shard_map/ppermute | solution.py:276
